TPU v7x, 512 devices: a whole 4x4x16 slice. The times are simulated.
512 devices in a mesh: vocab: 64 (over z, x_lo, core), hid: 8 (over x_hi, y).
Axes of the slice: x: 4 (x_hi: 2, x_lo: 2; x = x_hi * 2 + x_lo), y: 4, z: 16, core: 2. Of those that a mesh axis runs over, the one named last changes fastest.
Arguments:
- posterior: bfloat16 [512, 16384], P(None, 'vocab'), may hold values from 1.9e-09 to 1, as said below
- transition: bfloat16 [16384, 16384], P('vocab', 'hid'), may hold values from 1e-07 to 1, as said below
- emission: bfloat16 [16384, 16384], P('hid', 'vocab'), may hold values from 6e-06 to 90, as said below
- advance: bfloat16 [256, 16384], P(None, 'hid'), may hold values from 0.0099487305 to 1
- dfa_state: int32 [512], replicated, may hold values from 0 to 255
- edge_next: int32 [256, 8], replicated, may hold values from 0 to 255
- token_edge: int32 [256, 16384], P(None, 'vocab'), may hold values from 0 to 7
- allowed: int32 [512, 128], P(None, 'vocab'), may hold values from 0 to 1, as said below
Outputs:
- constrained_logprob: float32 [512, 16384], P('hid', 'vocab')
Inputs may be any that keep to these rules, and one draw needn't show every extreme that they name: `allowed`: every request allows at least one block. `posterior`: positive. `transition`: positive. `emission`: positive.
All inputs are finite; a program needn't handle non-finite values.
Results may differ from a plain program's by a relative error of at most 0.0015.
Values may be sent and summed in bfloat16 or wider, within the bound.
A program may use at most 64 MiB of HBM per device.

v0:
```python
import jax
import jax.numpy as jnp
from jax import lax
from jax.sharding import PartitionSpec as P

BLK = 128


def request_scores(prior_rows, dfa_state, edge_next, token_edge, allowed, advance, emission):
    row_count = prior_rows.shape[0]
    successor = jnp.take(edge_next, dfa_state, axis=0)
    look_rows = jnp.take(advance, successor, axis=0)
    weighted = (prior_rows.astype(jnp.float32)[:, None, :] * look_rows.astype(jnp.float32)).astype(
        jnp.bfloat16
    )
    slot_count = successor.shape[1]
    flattened = weighted.reshape(row_count * slot_count, weighted.shape[2])
    candidate = jnp.dot(flattened, emission, preferred_element_type=jnp.float32).reshape(
        row_count, slot_count, emission.shape[1]
    )
    edge_slots = jnp.take(token_edge, dfa_state, axis=0)
    labels = jnp.arange(slot_count, dtype=jnp.int32)
    chosen = jnp.sum(
        jnp.where(edge_slots[:, None, :] == labels[None, :, None], candidate, jnp.float32(0.0)),
        axis=1,
    )
    token_mask = jnp.repeat(allowed, BLK, axis=1)
    return jnp.where(token_mask > 0, chosen, jnp.float32(0.0))


def body(posterior, transition, emission, advance, dfa_state, edge_next, token_edge, allowed):
    prior_own = lax.psum_scatter(
        jnp.dot(posterior, transition, preferred_element_type=jnp.float32),
        "vocab",
        scatter_dimension=0,
        tiled=True,
    ).astype(jnp.bfloat16)
    partials = request_scores(
        lax.all_gather(prior_own, "vocab", axis=0, tiled=True),
        dfa_state,
        edge_next,
        token_edge,
        allowed,
        advance,
        emission,
    )
    scores = lax.psum_scatter(
        partials.astype(jnp.bfloat16), "hid", scatter_dimension=0, tiled=True
    ).astype(jnp.float32)
    local_rows = scores.shape[0]
    first_local = lax.axis_index("hid") * local_rows
    totals = lax.psum(jnp.sum(scores, axis=1), "vocab")
    mask_rows = lax.dynamic_slice_in_dim(allowed, first_local, local_rows, 0)
    token_mask = jnp.repeat(mask_rows, BLK, axis=1) > 0
    safe = jnp.where(token_mask, scores, jnp.float32(1.0))
    return jnp.where(token_mask, jnp.log(safe) - jnp.log(totals)[:, None], jnp.float32(0.0))


def solution(mesh):
    in_specs = (
        P(None, "vocab"),
        P("vocab", "hid"),
        P("hid", "vocab"),
        P(None, "hid"),
        P(),
        P(),
        P(None, "vocab"),
        P(None, "vocab"),
    )
    out_specs = P("hid", "vocab")
    return jax.shard_map(body, mesh=mesh, in_specs=in_specs, out_specs=out_specs, check_vma=False)
```

profile of v0, /device:TPU:4, one launch (start us, length us, event | category | flops | bytes accessed | tf_op | source)
XLA Modules:
  0.0 602.1 jit_solution(13615866778587981965)
XLA Ops:
  6.5 4.0 fusion.9
  10.7 236.6 %reduce-scatter.3.cloned.1.call-done = f32[8,2048]{1,0:T(8,128)} async-done(((f32[512,2048]{1,0:T(8,128)}), f32[8,2048]{1,0:T(8,128)}) %reduce-scatter.3.cloned.1.call-update) | async-done | bytes 65552 | tf_op jit(solution)/shard_map/reduce_scatter | solution.py:32
  247.2 1.5 convert_element_type.22
  248.8 0.7 broadcast_compare_fusion
  249.5 0.3 copy.18
  249.8 0.8 copy.15
  250.6 0.7 compare_select_fusion.2
  251.3 1.0 gather_fusion.1
  252.3 0.7 compare_and_fusion.1
  253.0 0.2 compare_and_fusion
  253.3 0.1 compare_select_fusion
  253.4 0.1 reshape.104
  253.6 1.6 gather_fusion
  255.2 21.0 %gather_fusion.2 = bf16[4096,2048]{1,0:T(8,128)(2,1)} fusion(bf16[256,2048]{1,0:T(8,128)(2,1)S(1)} %copy-done, s32[4096]{0:T(1024)S(1)} %broadcast_clamp_fusion), kind=kCustom, calls=%fused_computation.2 | custom fusion | bytes 33570816 | tf_op jit(solution)/shard_map/jit(_take)/gather | solution.py:12
  276.3 91.9 %all-gather.2.cloned.1.call-done = bf16[512,2048]{1,0:T(8,128)(2,1)} async-done(((bf16[8,2048]{1,0:T(8,128)(2,1)}), bf16[512,2048]{1,0:T(8,128)(2,1)}) %all-gather.2.cloned.1.call-update) | async-done | bytes 2097168 | tf_op jit(solution)/shard_map/all_gather | solution.py:39
  368.2 2.1 convert_element_type.23
  370.3 33.8 %select_reduce_fusion = bf16[512,256]{1,0:T(8,128)(2,1)S(1)} fusion(s32[512,256]{1,0:T(8,128)S(1)} %broadcast_select_fusion, bf16[512,8,2048]{2,1,0:T(8,128)(2,1)} %bitcast.16, f32[512,2048]{1,0:T(8,128)S(1)} %convert_element_type.23, pred[512,8]{0,1:T(8,128)(4,1)S(1)} %copy.16, bf16[2048,256]{1,0:T(8,128)(2,1)S(1)} %copy-done.2), kind=kOutput, calls=%fused_computation.9 | convolution fusion | flops 4331536384 | bytes 22810624 | tf_op jit(solution)/shard_map/dot_general | solution.py:18
  404.2 0.8 select_convert_fusion
  405.0 0.8 dynamic-slice_compare_fusion
  405.8 80.3 %reduce-scatter.5.cloned.1.call-done = bf16[64,256]{1,0:T(8,128)(2,1)} async-done(((bf16[512,256]{1,0:T(8,128)(2,1)}), bf16[64,256]{1,0:T(8,128)(2,1)}) %reduce-scatter.5.cloned.1.call-update) | async-done | bytes 32784 | tf_op jit(solution)/shard_map/reduce_scatter | solution.py:47
  486.2 0.9 convert_reduce_fusion
  487.0 106.9 %psum.7 = f32[64]{0:T(128)S(1)} all-reduce(f32[64]{0:T(128)S(1)} %convert_reduce_fusion), channel_id=1, replica_groups=mesh['vocab'=64,'hid'=8] {'vocab'}, use_global_device_ids=true, to_apply=%region_4.5 | all-reduce | flops 64 | bytes 512 | tf_op jit(solution)/shard_map/psum | solution.py:52
  593.9 0.1 broadcast_in_dim.61
  594.1 1.5 fusion.7
  (19 shorter events, 0.6 us)
Async XLA Ops:
  6.5 248.7 %copy-start = (bf16[256,2048]{1,0:T(8,128)(2,1)S(1)}, bf16[256,2048]{1,0:T(8,128)(2,1)}, u32[]{:S(2)}) copy-start(bf16[256,2048]{1,0:T(8,128)(2,1)} %param.11) | copy-start | bytes 3145732
  6.5 247.1 %copy-start.1 = (s32[256,256]{1,0:T(8,128)S(1)}, s32[256,256]{1,0:T(8,128)}, u32[]{:S(2)}) copy-start(s32[256,256]{1,0:T(8,128)} %param.14) | copy-start | bytes 786436
  6.5 240.7 %reduce-scatter.3.cloned.1.call-start = ((), (), s32[]{:S(2)}) async-start(), calls=%async_computation.2 | async-start | bytes 4259840 | tf_op jit(solution)/shard_map/reduce_scatter | solution.py:32
  10.6 357.6 %all-gather.2.cloned.1.call-start = ((), (), s32[]{:S(2)}) async-start(), calls=%async_computation.3 | async-start | bytes 2129920 | tf_op jit(solution)/shard_map/all_gather | solution.py:39
  248.7 237.5 %reduce-scatter.5.cloned.1.call-start = ((), (), s32[]{:S(2)}) async-start(), calls=%async_computation.4 | async-start | bytes 294912 | tf_op jit(solution)/shard_map/reduce_scatter | solution.py:47
  255.2 115.1 %copy-start.2 = (bf16[2048,256]{1,0:T(8,128)(2,1)S(1)}, bf16[2048,256]{1,0:T(8,128)(2,1)}, u32[]{:S(2)}) copy-start(bf16[2048,256]{1,0:T(8,128)(2,1)} %param.10) | copy-start | bytes 3145732
Sparse Core Ops, SparseCore 0:
  10.7 236.4 reduce-scatter.2
  249.6 118.5 all-gather.1
  405.1 81.0 reduce-scatter.4
where the time goes:
time: 603 us; the launch traced here: 602 us
  waiting for transfers between devices  409 us (68%)
  blocking collectives  107 us (18%)
  matrix products  37.9 us (6%)
  local copies, waits for them, and re-layouts  25.2 us (4%)
  between operations  13.2 us (2%)
  other arithmetic  9.95 us (2%)
    reduce_scatter x1, waiting for transfers between devices, body(): lax.psum_scatter(jnp.dot(posterior, transition, preferred_element_type=jn...  237 us
    psum x1, blocking collectives, body(): totals = lax.psum(jnp.sum(scores, axis=1), 'vocab')  107 us
    all_gather x1, waiting for transfers between devices, body(): lax.all_gather(prior_own, 'vocab', axis=0, tiled=True)  91.9 us
    reduce_scatter x1, waiting for transfers between devices, body(): lax.psum_scatter(partials.astype(jnp.bfloat16), 'hid', scatter_dimension=...  80.3 us
    dot_general x1, matrix products, request_scores(): jnp.dot(flattened, emission, preferred_element_type=jnp.float32)  33.8 us
    gather x1, local copies, waits for them, and re-layouts, request_scores(): look_rows = jnp.take(advance, successor, axis=0)  21 us
  transfers between devices with their start and end apart: 3, of which 3 were waited for; matrix products, arithmetic and copies ran while one was open for 5% of the time, Pallas kernels for 0%

commit v1 on v0

--- a/solution.py
+++ b/solution.py
@@ -2,6 +2,7 @@
 import jax.numpy as jnp
 from jax import lax
 from jax.sharding import PartitionSpec as P
+from jax.lax import all_gather
 
 BLK = 128
 
@@ -49,7 +50,8 @@
     ).astype(jnp.float32)
     local_rows = scores.shape[0]
     first_local = lax.axis_index("hid") * local_rows
-    totals = lax.psum(jnp.sum(scores, axis=1), "vocab")
+    inputs = jnp.sum(scores, axis=1)
+    totals = jnp.sum(all_gather(inputs, "vocab"), axis=0)
     mask_rows = lax.dynamic_slice_in_dim(allowed, first_local, local_rows, 0)
     token_mask = jnp.repeat(mask_rows, BLK, axis=1) > 0
     safe = jnp.where(token_mask, scores, jnp.float32(1.0))

time: 603 us -> 706 us (1.17)
  blocking collectives: 107 us -> 210 us
    unnamed x0 -> x1, blocking collectives: none -> 210 us
    psum x1 -> x0, blocking collectives: 107 us -> none  [body(): totals = lax.psum(jnp.sum(scores, axis=1), 'vocab')]
  transfers between devices with their start and end apart: 3 -> 3, of which waited for: 3 -> 3; matrix products, arithmetic and copies ran while one was open for 5% -> 4% of each run, Pallas kernels for 0% -> 0%
where the time goes in v1:
time: 706 us; the launch traced here: 705 us
  waiting for transfers between devices  407 us (58%)
  blocking collectives  210 us (30%)
  matrix products  37.9 us (5%)
  local copies, waits for them, and re-layouts  26.8 us (4%)
  between operations  13.9 us (2%)
  other arithmetic  9.98 us (1%)
    reduce_scatter x1, waiting for transfers between devices, body(): lax.psum_scatter(jnp.dot(posterior, transition, preferred_element_type=jn...  237 us
    unnamed x1, blocking collectives  210 us
    all_gather x1, waiting for transfers between devices, body(): lax.all_gather(prior_own, 'vocab', axis=0, tiled=True)  91.9 us
    reduce_scatter x1, waiting for transfers between devices, body(): lax.psum_scatter(partials.astype(jnp.bfloat16), 'hid', scatter_dimension=...  78.4 us
    dot_general x1, matrix products, request_scores(): jnp.dot(flattened, emission, preferred_element_type=jnp.float32)  33.8 us
    gather x1, local copies, waits for them, and re-layouts, request_scores(): look_rows = jnp.take(advance, successor, axis=0)  21 us
  transfers between devices with their start and end apart: 3, of which 3 were waited for; matrix products, arithmetic and copies ran while one was open for 4% of the time, Pallas kernels for 0%

profile of v1, /device:TPU:4, one launch (start us, length us, event | category | flops | bytes accessed | tf_op | source)
XLA Modules:
  0.0 705.1 jit_solution(18434296811761582645)
XLA Ops:
  6.5 4.0 fusion.9
  10.7 236.6 %reduce-scatter.3.cloned.1.call-done = f32[8,2048]{1,0:T(8,128)} async-done(((f32[512,2048]{1,0:T(8,128)}), f32[8,2048]{1,0:T(8,128)}) %reduce-scatter.3.cloned.1.call-update) | async-done | bytes 65552 | tf_op jit(solution)/shard_map/reduce_scatter | solution.py:33
  247.2 1.5 convert_element_type.22
  248.8 0.7 broadcast_compare_fusion
  249.5 0.3 copy.23
  249.8 0.8 copy.20
  250.6 0.7 compare_select_fusion.2
  251.3 1.0 gather_fusion.1
  252.3 0.7 compare_and_fusion.1
  253.0 0.2 compare_and_fusion
  253.4 0.1 reshape.106
  253.6 1.6 gather_fusion
  255.2 21.0 %gather_fusion.2 = bf16[4096,2048]{1,0:T(8,128)(2,1)} fusion(bf16[256,2048]{1,0:T(8,128)(2,1)S(1)} %copy-done, s32[4096]{0:T(1024)S(1)} %broadcast_clamp_fusion), kind=kCustom, calls=%fused_computation.2 | custom fusion | bytes 33570816 | tf_op jit(solution)/shard_map/jit(_take)/gather | solution.py:13
  276.3 91.9 %all-gather.3.cloned.1.call-done = bf16[512,2048]{1,0:T(8,128)(2,1)} async-done(((bf16[8,2048]{1,0:T(8,128)(2,1)}), bf16[512,2048]{1,0:T(8,128)(2,1)}) %all-gather.3.cloned.1.call-update) | async-done | bytes 2097168 | tf_op jit(solution)/shard_map/all_gather | solution.py:40
  368.2 2.1 convert_element_type.23
  370.3 33.8 %select_reduce_fusion = bf16[512,256]{1,0:T(8,128)(2,1)S(1)} fusion(s32[512,256]{1,0:T(8,128)S(1)} %broadcast_select_fusion, bf16[512,8,2048]{2,1,0:T(8,128)(2,1)} %bitcast.17, f32[512,2048]{1,0:T(8,128)S(1)} %convert_element_type.23, pred[512,8]{0,1:T(8,128)(4,1)S(1)} %copy.21, bf16[2048,256]{1,0:T(8,128)(2,1)S(1)} %copy-done.2), kind=kOutput, calls=%fused_computation.9 | convolution fusion | flops 4331536384 | bytes 22810624 | tf_op jit(solution)/shard_map/dot_general | solution.py:19
  404.2 0.8 select_convert_fusion
  405.0 0.8 dynamic-slice_compare_fusion
  405.8 1.3 dynamic-slice
  407.8 78.4 %reduce-scatter.5.cloned.1.call-done = bf16[64,256]{1,0:T(8,128)(2,1)} async-done(((bf16[512,256]{1,0:T(8,128)(2,1)}), bf16[64,256]{1,0:T(8,128)(2,1)}) %reduce-scatter.5.cloned.1.call-update) | async-done | bytes 32784 | tf_op jit(solution)/shard_map/reduce_scatter | solution.py:48
  486.2 0.9 convert_reduce_fusion
  487.0 0.3 dynamic-update-slice
  487.3 209.6 %all-reduce = f32[4096]{0:T(1024)S(1)} all-reduce(f32[4096]{0:T(1024)S(1)} %dynamic-update-slice), channel_id=2, replica_groups=mesh['vocab'=64,'hid'=8] {'vocab'}, use_global_device_ids=true, to_apply=%add | all-reduce | flops 4096 | bytes 32768
  697.1 1.5 fusion.7
  (24 shorter events, 1.0 us)
Async XLA Ops:
  6.5 248.7 %copy-start = (bf16[256,2048]{1,0:T(8,128)(2,1)S(1)}, bf16[256,2048]{1,0:T(8,128)(2,1)}, u32[]{:S(2)}) copy-start(bf16[256,2048]{1,0:T(8,128)(2,1)} %param.11) | copy-start | bytes 3145732
  6.5 247.1 %copy-start.1 = (s32[256,256]{1,0:T(8,128)S(1)}, s32[256,256]{1,0:T(8,128)}, u32[]{:S(2)}) copy-start(s32[256,256]{1,0:T(8,128)} %param.14) | copy-start | bytes 786436
  6.5 240.7 %reduce-scatter.3.cloned.1.call-start = ((), (), s32[]{:S(2)}) async-start(), calls=%async_computation.2 | async-start | bytes 4259840 | tf_op jit(solution)/shard_map/reduce_scatter | solution.py:33
  10.6 357.6 %all-gather.3.cloned.1.call-start = ((), (), s32[]{:S(2)}) async-start(), calls=%async_computation.3 | async-start | bytes 2129920 | tf_op jit(solution)/shard_map/all_gather | solution.py:40
  248.7 237.5 %reduce-scatter.5.cloned.1.call-start = ((), (), s32[]{:S(2)}) async-start(), calls=%async_computation.4 | async-start | bytes 294912 | tf_op jit(solution)/shard_map/reduce_scatter | solution.py:48
  255.2 115.1 %copy-start.2 = (bf16[2048,256]{1,0:T(8,128)(2,1)S(1)}, bf16[2048,256]{1,0:T(8,128)(2,1)}, u32[]{:S(2)}) copy-start(bf16[2048,256]{1,0:T(8,128)(2,1)} %param.10) | copy-start | bytes 3145732
Sparse Core Ops, SparseCore 0:
  10.7 236.4 reduce-scatter.2
  249.6 118.5 all-gather.2
  405.1 81.0 reduce-scatter.4
